TPU v7x, 32 devices: a whole 2x2x4 slice. The times are simulated.
32 devices in a mesh: ctx: 8 (over z, x), head: 4 (over y, core).
Axes of the slice: x: 2, y: 2, z: 4, core: 2. Of those that a mesh axis runs over, the one named last changes fastest.
Arguments:
- query: bfloat16 [8192, 4096], P(('ctx', 'head')), may hold values from -90 to 90
- keys: bfloat16 [8192, 4096], P(('ctx', 'head')), may hold values from -4.5 to 4.5
- values: bfloat16 [8192, 4096], P(('ctx', 'head')), may hold values from -5 to 5
- grad_out: bfloat16 [8192, 4096], P(('ctx', 'head')), may hold values from -5 to 5
- random_owner: int32 [64, 3], replicated, may hold values from 0 to 7, all different within a row; in each aligned block of 8 rows (0 to 7, 8 to 15, ...) at most 4 rows name the same one
- random_within: int32 [64, 3], replicated, may hold values from 0 to 7
- global_ids: int32 [64, 2], replicated, may hold values from 0 to 3, all different within a row
Outputs:
- grad_query: bfloat16 [8192, 4096], P(('ctx', 'head'))
- grad_keys: bfloat16 [8192, 4096], P(('ctx', 'head'))
- grad_values: bfloat16 [8192, 4096], P(('ctx', 'head'))
Inputs may be any that keep to these rules, and one draw needn't show every extreme that they name: `random_owner`: in the 8 rows of one index of ctx no owner is named more than 4 times, a bound that some block reaches in some of them; the 3 owners of one row differ. `global_ids`: the 2 blocks of one row differ; every block 0 to 3 is named by some row.
All inputs are finite; a program needn't handle non-finite values.
Results may differ from a plain program's by a relative error of at most 0.0053.
Values may be sent and summed in bfloat16 or wider, within the bound.
A program may use at most 320 MiB of HBM per device.

v0:
```python
from functools import partial

import jax
import jax.numpy as jnp
from jax import lax
from jax.experimental import pallas as pl
from jax.experimental.pallas import tpu as pltpu
from jax.sharding import PartitionSpec as P


HEAD_DIM = 128
BLOCK = 128
RAND = 3
GLOB = 2
NGLOB = 4
SLOTS = 3 + GLOB + RAND
CHUNKS = 2
SCALE = HEAD_DIM ** (-0.5)
LOG2E = 1.4426950408889634
NEG = -1e30
VMEM_LIMIT = 60 * 1024 * 1024


def dot(a, b, dims):
    return lax.dot_general(a, b, (dims, ((), ())), preferred_element_type=jnp.float32)


def pack_kernel(own_idx, far_idx, *refs, groups):
    outs = refs[-groups:]
    for m in range(groups):
        outs[m][0, 0] = refs[2 * m][...]
        outs[m][1, 0] = refs[2 * m + 1][...]


def pack(own_idx, far_idx, kv, kv_far, ready, groups, cap):
    features = kv.shape[-1]
    block = (2, BLOCK, features)
    in_specs, args = [], []
    for m in range(groups):
        in_specs.append(pl.BlockSpec(block, lambda c, oi, fi, m=m: (0, oi[m * cap + c], 0)))
        in_specs.append(pl.BlockSpec(block, lambda c, oi, fi, m=m: (0, fi[m * cap + c], 0)))
        args += [kv, kv_far]
    in_specs += [pl.BlockSpec(memory_space=pl.ANY)] * len(ready)
    return pl.pallas_call(
        partial(pack_kernel, groups=groups),
        grid_spec=pltpu.PrefetchScalarGridSpec(
            num_scalar_prefetch=2,
            grid=(cap,),
            in_specs=in_specs,
            out_specs=[
                pl.BlockSpec((2, 1, 2, BLOCK, features), lambda c, *_: (0, c, 0, 0, 0))
            ] * groups,
        ),
        out_shape=[jax.ShapeDtypeStruct((2, cap, 2, BLOCK, features), kv.dtype)] * groups,
        compiler_params=pltpu.CompilerParams(vmem_limit_bytes=VMEM_LIMIT),
        name="pack",
    )(own_idx, far_idx, *args, *ready)


def attn_kernel(
    gid_ref,
    slot_ref,
    edge_ref,
    q_ref,
    g_ref,
    kv_ref,
    left_ref,
    right_ref,
    sum_ref,
    *refs,
    blocks,
    groups,
    each,
):
    incs, refs = refs[:groups], refs[groups:]
    dq_ref, own_ref, dleft_ref, dright_ref, dsum_ref = refs[:5]
    term_outs = refs[5 : 5 + groups]
    kwin, vwin, kcat, vcat, dkw, dvw, sacc, inc_ref, terms_ref = refs[5 + groups :]
    for m in range(groups):
        inc_ref[m * each : (m + 1) * each] = incs[m][...]
    rows = blocks * BLOCK
    for win, x in ((kwin, 0), (vwin, 1)):
        win[0:BLOCK] = left_ref[x]
        win[BLOCK : BLOCK + rows] = kv_ref[x]
        win[BLOCK + rows :] = right_ref[x]
    dkw[...] = jnp.zeros_like(dkw)
    dvw[...] = jnp.zeros_like(dvw)
    sacc[...] = jnp.zeros_like(sacc)
    terms_ref[...] = jnp.zeros_like(terms_ref)

    def step(i, carry):
        base = pl.multiple_of(i * BLOCK, BLOCK)
        here = pl.ds(base, BLOCK)
        window = pl.ds(base, 3 * BLOCK)
        kcat[0 : 3 * BLOCK] = kwin[window]
        vcat[0 : 3 * BLOCK] = vwin[window]
        for n in range(GLOB):
            gid = pl.multiple_of(gid_ref[i * GLOB + n] * BLOCK, BLOCK)
            at = slice((3 + n) * BLOCK, (4 + n) * BLOCK)
            kcat[at] = sum_ref[0, pl.ds(gid, BLOCK)]
            vcat[at] = sum_ref[1, pl.ds(gid, BLOCK)]
        for n in range(RAND):
            slot = slot_ref[i * RAND + n]
            at = slice((3 + GLOB + n) * BLOCK, (4 + GLOB + n) * BLOCK)
            kcat[at] = inc_ref[slot, 0]
            vcat[at] = inc_ref[slot, 1]
        q = q_ref[here]
        g = g_ref[here]
        keys = kcat[...]
        s = dot(keys, q, ((1,), (1,)))
        no_left = (i == 0) & (edge_ref[0] == 1)
        no_right = (i == blocks - 1) & (edge_ref[1] == 1)
        s = jnp.concatenate(
            [
                jnp.where(no_left, NEG, s[0:BLOCK]),
                s[BLOCK : 2 * BLOCK],
                jnp.where(no_right, NEG, s[2 * BLOCK : 3 * BLOCK]),
                s[3 * BLOCK :],
            ],
            axis=0,
        )
        highest = jnp.max(s, axis=0, keepdims=True)
        e = jnp.exp2((s - highest) * (SCALE * LOG2E))
        p = e * (1.0 / jnp.sum(e, axis=0, keepdims=True))
        dp = dot(vcat[...], g, ((1,), (1,)))
        row_dot = jnp.sum(p * dp, axis=0, keepdims=True)
        ds = (p * (dp - row_dot)).astype(jnp.bfloat16)
        p_low = p.astype(jnp.bfloat16)
        dq = dot(ds, keys, ((0,), (0,))) * SCALE
        dq_ref[here] = dq.astype(jnp.bfloat16)
        dk = dot(ds, q, ((1,), (0,))) * SCALE
        dv = dot(p_low, g, ((1,), (0,)))
        dkw[window] += dk[0 : 3 * BLOCK]
        dvw[window] += dv[0 : 3 * BLOCK]
        for n in range(GLOB):
            gid = pl.multiple_of(gid_ref[i * GLOB + n] * BLOCK, BLOCK)
            at = slice((3 + n) * BLOCK, (4 + n) * BLOCK)
            sacc[0, pl.ds(gid, BLOCK)] += dk[at]
            sacc[1, pl.ds(gid, BLOCK)] += dv[at]
        for n in range(RAND):
            slot = slot_ref[i * RAND + n]
            at = slice((3 + GLOB + n) * BLOCK, (4 + GLOB + n) * BLOCK)
            terms_ref[slot, 0] = dk[at].astype(jnp.bfloat16)
            terms_ref[slot, 1] = dv[at].astype(jnp.bfloat16)
        return carry

    lax.fori_loop(0, blocks, step, 0)
    for acc, x in ((dkw, 0), (dvw, 1)):
        dleft_ref[x] = acc[0:BLOCK].astype(jnp.bfloat16)
        own_ref[x] = acc[BLOCK : BLOCK + rows]
        dright_ref[x] = acc[BLOCK + rows :].astype(jnp.bfloat16)
    dsum_ref[...] = sacc[...].astype(jnp.bfloat16)
    for m in range(groups):
        term_outs[m][...] = terms_ref[m * each : (m + 1) * each]


def attention(gids, slots, edges, q, g, kv, left, right, summary, incoming):
    rows, features = q.shape
    blocks = rows // BLOCK
    groups = len(incoming)
    each = incoming[0].shape[0]
    col = lambda h, *_: (0, h)
    col3 = lambda h, *_: (0, 0, h)
    col4 = lambda h, *_: (0, 0, 0, h)
    tok = pl.BlockSpec((rows, HEAD_DIM), col)
    halo = pl.BlockSpec((2, BLOCK, HEAD_DIM), col3)
    summ = pl.BlockSpec((2, NGLOB * BLOCK, HEAD_DIM), col3)
    inc = pl.BlockSpec((each, 2, BLOCK, HEAD_DIM), col4)
    pair = pl.BlockSpec((2, rows, HEAD_DIM), col3)
    low = jnp.bfloat16
    wide = rows + 2 * BLOCK
    return pl.pallas_call(
        partial(attn_kernel, blocks=blocks, groups=groups, each=each),
        grid_spec=pltpu.PrefetchScalarGridSpec(
            num_scalar_prefetch=3,
            grid=(features // HEAD_DIM,),
            in_specs=[tok, tok, pair, halo, halo, summ] + [inc] * groups,
            out_specs=[
                tok,
                pair,
                halo,
                halo,
                summ,
            ]
            + [inc] * groups,
            scratch_shapes=[
                pltpu.VMEM((wide, HEAD_DIM), low),
                pltpu.VMEM((wide, HEAD_DIM), low),
                pltpu.VMEM((SLOTS * BLOCK, HEAD_DIM), low),
                pltpu.VMEM((SLOTS * BLOCK, HEAD_DIM), low),
                pltpu.VMEM((wide, HEAD_DIM), jnp.float32),
                pltpu.VMEM((wide, HEAD_DIM), jnp.float32),
                pltpu.VMEM((2, NGLOB * BLOCK, HEAD_DIM), jnp.float32),
                pltpu.VMEM((groups * each, 2, BLOCK, HEAD_DIM), low),
                pltpu.VMEM((groups * each, 2, BLOCK, HEAD_DIM), low),
            ],
        ),
        out_shape=[
            jax.ShapeDtypeStruct((rows, features), low),
            jax.ShapeDtypeStruct((2, rows, features), jnp.float32),
            jax.ShapeDtypeStruct((2, BLOCK, features), low),
            jax.ShapeDtypeStruct((2, BLOCK, features), low),
            jax.ShapeDtypeStruct((2, NGLOB * BLOCK, features), low),
        ]
        + [jax.ShapeDtypeStruct((each, 2, BLOCK, features), low)] * groups,
        compiler_params=pltpu.CompilerParams(vmem_limit_bytes=VMEM_LIMIT),
        name="attention",
    )(gids, slots, edges, q, g, kv, left, right, summary, *incoming)


def add_slots(acc, idx_ref, incs, cap):
    for m, inc in enumerate(incs):
        for c in range(cap):
            at = pl.ds(pl.multiple_of(idx_ref[m * cap + c] * BLOCK, BLOCK), BLOCK)
            acc[0, at] += inc[0, c, 0].astype(jnp.float32)
            acc[1, at] += inc[0, c, 1].astype(jnp.float32)


def far_kernel(idx_ref, *refs, groups, cap):
    sum_refs = refs[groups : 2 * groups]
    out_ref, total_ref, acc = refs[2 * groups :]
    acc[...] = jnp.zeros_like(acc)
    total = sum_refs[0][...].astype(jnp.float32)
    for ref in sum_refs[1:]:
        total += ref[...].astype(jnp.float32)
    total_ref[...] = total

    @pl.when(idx_ref[groups * cap] == 1)
    def _():
        acc[:, 0 : NGLOB * BLOCK] += total

    add_slots(acc, idx_ref, refs[:groups], cap)
    out_ref[...] = acc[...].astype(jnp.bfloat16)


def own_kernel(idx_ref, *refs, groups, cap):
    own_ref, far_ref, first_ref, last_ref, sum_ref, dk_ref, dv_ref, acc = refs[groups:]
    rows = own_ref.shape[1]
    acc[...] = own_ref[...] + far_ref[...].astype(jnp.float32)
    acc[:, 0:BLOCK] += first_ref[...].astype(jnp.float32)
    acc[:, rows - BLOCK :] += last_ref[...].astype(jnp.float32)

    @pl.when(idx_ref[groups * cap] == 1)
    def _():
        acc[:, 0 : NGLOB * BLOCK] += sum_ref[...]

    add_slots(acc, idx_ref, refs[:groups], cap)
    dk_ref[...] = acc[0].astype(jnp.bfloat16)
    dv_ref[...] = acc[1].astype(jnp.bfloat16)


def combine(kernel, side, idx, incoming, extra, rows, out_specs, out_shape):
    groups = len(incoming)
    cap = incoming[0].shape[1]
    features = incoming[0].shape[-1]
    col3 = lambda h, *_: (0, 0, h)
    spec3 = lambda x: pl.BlockSpec(x.shape[:2] + (HEAD_DIM,), col3)
    inc = pl.BlockSpec((1, cap, 2, BLOCK, HEAD_DIM), lambda h, *_: (side, 0, 0, 0, h))
    return pl.pallas_call(
        partial(kernel, groups=groups, cap=cap),
        grid_spec=pltpu.PrefetchScalarGridSpec(
            num_scalar_prefetch=1,
            grid=(features // HEAD_DIM,),
            in_specs=[inc] * groups + [spec3(x) for x in extra],
            out_specs=out_specs,
            scratch_shapes=[pltpu.VMEM((2, rows, HEAD_DIM), jnp.float32)],
        ),
        out_shape=out_shape,
        compiler_params=pltpu.CompilerParams(vmem_limit_bytes=VMEM_LIMIT),
    )(idx, *incoming, *extra)


def head_kernel(
    tab_ref,
    wt_ref,
    k_in,
    v_in,
    q_in,
    g_in,
    dq_out,
    dk_out,
    dv_out,
    kb,
    vb,
    qb,
    gb,
    dqb,
    dkb,
    dvb,
    dka,
    dva,
    terms_k,
    terms_v,
    run,
    kcat,
    vcat,
    in_send,
    in_recv,
    out_send,
    out_recv,
):
    heads = lax.axis_size("head")
    count = lax.axis_size("ctx") * heads
    half = count // 2
    me = lax.axis_index("ctx") * heads + lax.axis_index("head")
    mine = lax.div(me, half)
    each = k_in.shape[0]
    blocks = count * each
    entries = blocks * RAND
    at_gid, at_rid = 0, blocks * GLOB
    at_perm = at_rid + entries
    at_last = at_perm + entries
    at_carry = blocks * GLOB * NGLOB
    at_has = at_carry + entries

    def side(o):
        return lax.rem(mine + 1 + lax.div(o, half), 2) * half

    def target(o):
        return side(o) + lax.rem(me + lax.rem(o, half), half)

    def source(o):
        return side(o) + lax.rem(me + half - lax.rem(o, half), half)

    def coords(t):
        return (lax.div(t, heads), lax.rem(t, heads))

    def rows_of(s):
        return pl.ds(s * each, each)

    def rows_padded(s):
        return pl.ds(s * each + 1, each)

    def cols_of(s):
        return pl.ds(pl.multiple_of(s * HEAD_DIM, HEAD_DIM), HEAD_DIM)

    ins = ((k_in, kb, rows_padded), (v_in, vb, rows_padded), (q_in, qb, rows_of), (g_in, gb, rows_of))
    outs = ((dqb, dq_out), (dvb, dv_out), (dkb, dk_out))

    def bring(a, t, s):
        x, y, rows = ins[a]
        return pltpu.make_async_remote_copy(
            src_ref=x.at[:, :, cols_of(t)],
            dst_ref=y.at[rows(s)],
            send_sem=in_send.at[a, t],
            recv_sem=in_recv.at[a, s],
            device_id=coords(t),
            device_id_type=pl.DeviceIdType.MESH,
        )

    def bring_own(a):
        x, y, rows = ins[a]
        return pltpu.make_async_copy(x.at[:, :, cols_of(me)], y.at[rows(me)], in_recv.at[a, me])

    def give(a, t, s):
        x, y = outs[a]
        return pltpu.make_async_remote_copy(
            src_ref=x.at[rows_of(t)],
            dst_ref=y.at[:, :, cols_of(s)],
            send_sem=out_send.at[a, t],
            recv_sem=out_recv.at[a, s],
            device_id=coords(t),
            device_id_type=pl.DeviceIdType.MESH,
        )

    def give_own(a):
        x, y = outs[a]
        return pltpu.make_async_copy(x.at[rows_of(me)], y.at[:, :, cols_of(me)], out_recv.at[a, me])

    def peers(body):
        def run_body(o, carry):
            body(o)
            return carry

        lax.fori_loop(0, half, run_body, 0)
        lax.fori_loop(half + 1, count, run_body, 0)

    barrier = pltpu.get_barrier_semaphore()
    peers(
        lambda o: pl.semaphore_signal(
            barrier, inc=1, device_id=coords(target(o)), device_id_type=pl.DeviceIdType.MESH
        )
    )
    pl.semaphore_wait(barrier, count - 1)

    for pair in ((0, 1), (2, 3)):
        for a in pair:
            bring_own(a).start()

        def start(o):
            for a in pair:
                bring(a, target(o), me).start()

        peers(start)

    edge = jnp.zeros((BLOCK, HEAD_DIM), jnp.bfloat16)
    for ref in (kb, vb):
        ref[0] = edge
        ref[blocks + 1] = edge
    dka[...] = jnp.zeros_like(dka)
    dva[...] = jnp.zeros_like(dva)

    for a in (0, 1):
        bring_own(a).wait()
        peers(lambda o: bring(a, source(o), source(o)).wait_recv())

    def block_step(i):
        for n in range(3):
            at = slice(n * BLOCK, (n + 1) * BLOCK)
            kcat[at] = kb[i + n]
            vcat[at] = vb[i + n]
        gids = [tab_ref[at_gid + i * GLOB + n] for n in range(GLOB)]
        for n in range(GLOB + RAND):
            if n < GLOB:
                named = gids[n]
            else:
                named = tab_ref[at_rid + i * RAND + n - GLOB]
            at = slice((3 + n) * BLOCK, (4 + n) * BLOCK)
            kcat[at] = kb[named + 1]
            vcat[at] = vb[named + 1]
        q = qb[i]
        g = gb[i]
        keys = kcat[...]
        s = dot(keys, q, ((1,), (1,)))
        s = jnp.concatenate(
            [
                jnp.where(i == 0, NEG, s[0:BLOCK]),
                s[BLOCK : 2 * BLOCK],
                jnp.where(i == blocks - 1, NEG, s[2 * BLOCK : 3 * BLOCK]),
                s[3 * BLOCK :],
            ],
            axis=0,
        )
        highest = jnp.max(s, axis=0, keepdims=True)
        e = jnp.exp2((s - highest) * (SCALE * LOG2E))
        p = e * (1.0 / jnp.sum(e, axis=0, keepdims=True))
        dp = dot(vcat[...], g, ((1,), (1,)))
        row_dot = jnp.sum(p * dp, axis=0, keepdims=True)
        ds = (p * (dp - row_dot)).astype(jnp.bfloat16)
        p_low = p.astype(jnp.bfloat16)
        dq = dot(ds, keys, ((0,), (0,))) * SCALE
        dqb[i] = dq.astype(jnp.bfloat16)
        dk = dot(ds, q, ((1,), (0,))) * SCALE
        dv = dot(p_low, g, ((1,), (0,)))
        for n in range(3):
            at = slice(n * BLOCK, (n + 1) * BLOCK)
            dka[i + n] += dk[at]
            dva[i + n] += dv[at]
        for acc, x in ((dka, dk), (dva, dv)):
            for m in range(NGLOB):
                total = acc[m + 1]
                for n in range(GLOB):
                    at = slice((3 + n) * BLOCK, (4 + n) * BLOCK)
                    total += x[at] * wt_ref[((i * GLOB + n) * NGLOB) + m]
                acc[m + 1] = total
        for n in range(RAND):
            at = slice((3 + GLOB + n) * BLOCK, (4 + GLOB + n) * BLOCK)
            terms_k[i * RAND + n] = dk[at].astype(jnp.bfloat16)
            terms_v[i * RAND + n] = dv[at].astype(jnp.bfloat16)

    def attend(o, carry):
        s = source(o)

        @pl.when(o != half)
        def _():
            bring(2, s, s).wait_recv()
            bring(3, s, s).wait_recv()

        @pl.when(o == half)
        def _():
            bring_own(2).wait()
            bring_own(3).wait()

        def inner(b, c):
            block_step(s * each + b)
            return c

        lax.fori_loop(0, each, inner, 0)

        @pl.when(o != half)
        def _():
            give(0, s, me).start()

        @pl.when(o == half)
        def _():
            give_own(0).start()

        return carry

    lax.fori_loop(0, count, attend, 0)

    for a, terms, acc, low in ((1, terms_v, dva, dvb), (2, terms_k, dka, dkb)):

        def scan(e, total):
            total = total * wt_ref[at_carry + e] + terms[tab_ref[at_perm + e]].astype(jnp.float32)
            run[e] = total
            return total

        lax.fori_loop(0, entries, scan, jnp.zeros((BLOCK, HEAD_DIM), jnp.float32))

        def finish(o, carry):
            s = source(o)

            def inner(b, c):
                j = s * each + b
                total = run[tab_ref[at_last + j]] * wt_ref[at_has + j]
                low[j] = (total + acc[j + 1]).astype(jnp.bfloat16)
                return c

            lax.fori_loop(0, each, inner, 0)

            @pl.when(o != half)
            def _():
                give(a, s, me).start()

            @pl.when(o == half)
            def _():
                give_own(a).start()

            return carry

        lax.fori_loop(0, count, finish, 0)

    for a in range(4):
        peers(lambda o: bring(a, target(o), me).wait_send())
    for a in range(3):
        give_own(a).wait()

        def close(o):
            give(a, source(o), me).wait_send()
            give(a, source(o), source(o)).wait_recv()

        peers(close)


def attend_by_head(query, keys, values, grad_out, random_owner, random_within, global_ids):
    count = lax.axis_size("ctx") * lax.axis_size("head")
    tokens, width = query.shape
    rows = tokens * count
    blocks = rows // BLOCK
    entries = blocks * RAND
    low = jnp.bfloat16
    per_owner = blocks // lax.axis_size("ctx")
    named = (random_owner * per_owner + random_within).reshape(-1)
    ids = jnp.arange(entries, dtype=jnp.int32)
    order = named * entries + ids
    rank = jnp.sum((order[None, :] < order[:, None]).astype(jnp.int32), axis=1)
    hit = rank[None, :] == ids[:, None]
    perm = jnp.sum(jnp.where(hit, ids[None, :], 0), axis=1)
    before = jnp.sum((named[None, :] < named[:, None]).astype(jnp.int32), axis=1)
    start = jnp.sum(jnp.where(hit & (before == rank)[None, :], 1, 0), axis=1)
    keys_at = jnp.arange(blocks, dtype=jnp.int32)
    last = jnp.sum((named[None, :] <= keys_at[:, None]).astype(jnp.int32), axis=1) - 1
    has = jnp.any(named[None, :] == keys_at[:, None], axis=1).astype(jnp.int32)
    tab = jnp.concatenate(
        [global_ids.reshape(-1), named, perm, jnp.maximum(last, 0)]
    ).astype(jnp.int32)
    tops = jnp.arange(NGLOB, dtype=jnp.int32)
    picks = (global_ids.reshape(-1)[:, None] == tops).astype(jnp.int32).reshape(-1)
    weights = jnp.concatenate([picks, 1 - start, has]).astype(jnp.float32)
    any_spec = pl.BlockSpec(memory_space=pl.ANY)
    vmem = pltpu.VMEM
    held = lambda n, dtype: vmem((n, BLOCK, HEAD_DIM), dtype)
    in_blocks = lambda x: x.reshape(tokens // BLOCK, BLOCK, width)
    dma = pltpu.SemaphoreType.DMA
    outs = pl.pallas_call(
        head_kernel,
        in_specs=[pl.BlockSpec(memory_space=pltpu.SMEM)] * 2 + [any_spec] * 4,
        out_specs=[any_spec] * 3,
        out_shape=[jax.ShapeDtypeStruct((tokens // BLOCK, BLOCK, width), low)] * 3,
        scratch_shapes=[
            held(blocks + 2, low),
            held(blocks + 2, low),
            held(blocks, low),
            held(blocks, low),
            held(blocks, low),
            held(blocks, low),
            held(blocks, low),
            held(blocks + 2, jnp.float32),
            held(blocks + 2, jnp.float32),
            held(entries, low),
            held(entries, low),
            held(entries, jnp.float32),
            vmem((SLOTS * BLOCK, HEAD_DIM), low),
            vmem((SLOTS * BLOCK, HEAD_DIM), low),
            dma((4, count)),
            dma((4, count)),
            dma((3, count)),
            dma((3, count)),
        ],
        compiler_params=pltpu.CompilerParams(
            collective_id=0, has_side_effects=True, vmem_limit_bytes=VMEM_LIMIT
        ),
        name="head_attention",
    )(tab, weights, *[in_blocks(x) for x in (keys, values, query, grad_out)])
    return tuple(x.reshape(tokens, width) for x in outs)


def on_device(*args):
    devices = lax.axis_size("ctx") * lax.axis_size("head")
    if args[0].shape[1] == devices * HEAD_DIM and devices % 2 == 0:
        return attend_by_head(*args)
    return exchange_and_attend(*args)


def exchange_and_attend(query, keys, values, grad_out, random_owner, random_within, global_ids):
    ctx_count = lax.axis_size("ctx")
    head_count = lax.axis_size("head")
    ctx = lax.axis_index("ctx")
    tokens_in, width_all = query.shape
    features = width_all // head_count
    rows = tokens_in * head_count
    blocks = rows // BLOCK
    half = ctx_count // 2
    place = lax.rem(ctx, half)
    partner = lax.rem(ctx + half, ctx_count)
    flips = jnp.bitwise_xor(place, jnp.arange(half, dtype=jnp.int32))
    swap = [(i, (i + half) % ctx_count) for i in range(ctx_count)]
    up = [(i, i + 1) for i in range(ctx_count - 1)]
    down = [(i + 1, i) for i in range(ctx_count - 1)]
    entries = blocks * RAND
    cap = max(1, (4 * blocks * RAND + 3 * ctx_count - 1) // (3 * ctx_count))

    owner_all = random_owner.reshape(ctx_count, entries)
    within_all = random_within.reshape(ctx_count, entries)
    ids = jnp.arange(entries, dtype=jnp.int32)
    same = owner_all[:, :, None] == owner_all[:, None, :]
    rank_all = jnp.sum(
        jnp.where(same & (ids[None, :] < ids[:, None])[None], 1, 0), axis=2
    ).astype(jnp.int32)
    first = ctx - place
    owner_half = lax.dynamic_slice_in_dim(owner_all, first, half, 0)
    within_rows = lax.dynamic_slice_in_dim(within_all, first, half, 0)
    rank_half = lax.dynamic_slice_in_dim(rank_all, first, half, 0)
    caps = jnp.arange(cap, dtype=jnp.int32)

    def listed(owner):
        hit = (owner_half == owner)[:, :, None] & (rank_half[:, :, None] == caps)
        return jnp.sum(jnp.where(hit, within_rows[:, :, None], 0), axis=1)[flips].reshape(-1)

    own_idx = listed(ctx)
    far_idx = listed(partner)
    owner_mine = lax.dynamic_index_in_dim(owner_all, ctx, 0, keepdims=False)
    rank_mine = lax.dynamic_index_in_dim(rank_all, ctx, 0, keepdims=False)
    far_side = jnp.where(owner_mine // half == ctx // half, 0, 1)
    slots = (jnp.bitwise_xor(owner_mine % half, place) * 2 + far_side) * cap + rank_mine
    gids = lax.dynamic_slice_in_dim(global_ids, ctx * blocks, blocks, 0).reshape(-1)
    edges = jnp.stack([ctx == 0, ctx == ctx_count - 1]).astype(jnp.int32)
    far_flag = (partner == 0).astype(jnp.int32).reshape(1)
    own_flag = (ctx == 0).astype(jnp.int32).reshape(1)
    part = features // CHUNKS

    def to_heads(x, c):
        x = x.reshape(tokens_in, head_count, CHUNKS, part)[:, :, c].reshape(tokens_in, -1)
        return lax.all_to_all(x, "head", split_axis=1, concat_axis=0, tiled=True)

    def to_tokens(parts):
        back = [
            lax.all_to_all(x, "head", split_axis=0, concat_axis=1, tiled=True) for x in parts
        ]
        back = [x.reshape(tokens_in, head_count, part) for x in back]
        return jnp.stack(back, axis=2).reshape(tokens_in, width_all)

    stages = range(CHUNKS)
    kv, kv_far, q, g, incoming = {}, {}, {}, {}, {}
    left, right, summary = {}, {}, {}
    sums, dq, dsum, arrived, firsts, lasts, own, far = {}, {}, {}, {}, {}, {}, {}, {}
    outs = ([], [], [])
    top = NGLOB * BLOCK

    def spread(x):
        found = x
        for d in range(1, half):
            got = lax.ppermute(x, "ctx", [(a * half, a * half + d) for a in range(2)])
            found = jnp.where(place == d, got, found)
        return found

    def collect(x):
        return [
            lax.ppermute(x, "ctx", [(a * half + d, a * half) for a in range(2)])
            for d in range(1, half)
        ]

    def within_half(parts):
        return [parts[0]] + [
            lax.ppermute(
                parts[m],
                "ctx",
                [(i, i // half * half + (i % half ^ m)) for i in range(ctx_count)],
            )
            for m in range(1, half)
        ]

    def fetch(c):
        kv[c] = jnp.stack([to_heads(keys, c), to_heads(values, c)])
        kv_far[c] = lax.ppermute(kv[c], "ctx", swap)
        left[c] = lax.ppermute(kv[c][:, rows - BLOCK :], "ctx", up)
        right[c] = lax.ppermute(kv[c][:, :BLOCK], "ctx", down)
        q[c] = to_heads(query, c)
        g[c] = to_heads(grad_out, c)

    def route(c):
        summary[c] = spread(jnp.where(ctx < half, kv[c][:, :top], kv_far[c][:, :top]))
        ready = (left[c], right[c])
        packed = pack(own_idx, far_idx, kv[c], kv_far[c], ready, half, cap)
        incoming[c] = within_half(packed)

    def attend(c):
        flat = [x.reshape((2 * cap, 2, BLOCK, part)) for x in incoming[c]]
        dq[c], own[c], dleft, dright, dsum[c], *terms = attention(
            gids, slots, edges, q[c], g[c], kv[c], left[c], right[c], summary[c], flat
        )
        sums[c] = [dsum[c]] + collect(dsum[c])
        arrived[c] = within_half([x.reshape((2, cap, 2, BLOCK, part)) for x in terms])
        lasts[c] = lax.ppermute(dleft, "ctx", down)
        firsts[c] = lax.ppermute(dright, "ctx", up)

    def give_back(c):
        col3 = lambda h, *_: (0, 0, h)
        partial_far, dsum[c] = combine(
            far_kernel, 1, jnp.concatenate([far_idx, far_flag]), arrived[c], sums[c], rows,
            [
                pl.BlockSpec((2, rows, HEAD_DIM), col3),
                pl.BlockSpec((2, top, HEAD_DIM), col3),
            ],
            [
                jax.ShapeDtypeStruct((2, rows, part), jnp.bfloat16),
                jax.ShapeDtypeStruct((2, top, part), jnp.float32),
            ],
        )
        far[c] = lax.ppermute(partial_far, "ctx", swap)

    def finish(c):
        tok = pl.BlockSpec((rows, HEAD_DIM), lambda h, *_: (0, h))
        tok_shape = jax.ShapeDtypeStruct((rows, part), jnp.bfloat16)
        dk, dv = combine(
            own_kernel, 0, jnp.concatenate([own_idx, own_flag]), arrived[c],
            (own[c], far[c], firsts[c], lasts[c], dsum[c]),
            rows, [tok, tok], [tok_shape, tok_shape],
        )
        for out, x in zip(outs, (dq[c], dk, dv)):
            out.append(x)

    for step in (fetch, route, attend, give_back, finish):
        for c in stages:
            step(c)
    return tuple(to_tokens(x) for x in outs)


def solution(mesh):
    token = P(("ctx", "head"), None)
    return jax.shard_map(
        on_device,
        mesh=mesh,
        in_specs=(token, token, token, token, P(), P(), P()),
        out_specs=(token, token, token),
        check_vma=False,
    )
```

profile of v0, /device:TPU:27, one launch (start us, length us, event | category | flops | bytes accessed | tf_op | source)
XLA Modules:
  0.0 378.4 jit_solution(8497692743194695260)
XLA Ops:
  0.6 0.7 multiply_add_fusion
  1.3 0.1 copy.14
  1.4 0.1 reshape.67
  1.6 0.1 fusion.2
  1.7 0.1 convert_reduce_fusion.2
  1.8 0.2 convert_reduce_fusion
  2.1 0.2 select_reduce_fusion
  2.3 0.8 copy.13
  3.1 0.1 reshape.66
  3.2 0.7 pad_add_fusion.tab_ref
  3.9 0.1 fusion.1
  4.0 0.1 reshape.75
  4.1 0.7 add_convert_fusion.wt_ref
  4.7 366.7 %head_attention.1 = (bf16[2,128,4096]{2,1,0:T(8,128)(2,1)}, bf16[2,128,4096]{2,1,0:T(8,128)(2,1)}, bf16[2,128,4096]{2,1,0:T(8,128)(2,1)}) custom-call(s32[576]{0:T(1024)} %pad_add_fusion.tab_ref, f32[768]{0:T(1024)} %add_convert_fusion.wt_ref, bf16[2,128,4096]{2,1,0:T(8,128)(2,1)} %bitcast.7, bf16[2,128,4096]{2,1,0:T(8,128)(2,1)} %bitcast.8, ...), custom_call_target="tpu_custom_call" | custom-call | tf_op jit(solution)/shard_map/head_attention/pallas_call | solution.py:566
  371.4 0.0 copy-start.1
  371.4 3.3 copy.18
  374.7 0.0 copy-done.1
  374.7 0.0 copy-start
  374.7 1.3 copy.19
  376.0 1.0 copy-done
  377.1 1.3 copy.20
  (5 shorter events, 0.0 us)
Async XLA Ops:
  371.4 3.3 copy-start.1
  374.7 2.3 copy-start
where the time goes:
time: 379 us; the launch traced here: 378 us
  Pallas kernels  367 us (97%)
  local copies, waits for them, and re-layouts  8.19 us (2%)
    pallas_call x1, Pallas kernels, attend_by_head(): pl.pallas_call(head_kernel, in_specs=[pl.BlockSpec(memory_space=pltpu.SME...  367 us
    unnamed x8, local copies, waits for them, and re-layouts  7.72 us

commit v1 on v0

--- a/solution.py
+++ b/solution.py
@@ -314,13 +314,13 @@
     at_has = at_carry + entries
 
     def side(o):
-        return lax.rem(mine + 1 + lax.div(o, half), 2) * half
+        return lax.rem(mine + 1 + o, 2) * half
 
     def target(o):
-        return side(o) + lax.rem(me + lax.rem(o, half), half)
+        return side(o) + lax.rem(me + lax.div(o, 2), half)
 
     def source(o):
-        return side(o) + lax.rem(me + half - lax.rem(o, half), half)
+        return side(o) + lax.rem(me + half - lax.div(o, 2), half)
 
     def coords(t):
         return (lax.div(t, heads), lax.rem(t, heads))
@@ -372,8 +372,8 @@
             body(o)
             return carry
 
-        lax.fori_loop(0, half, run_body, 0)
-        lax.fori_loop(half + 1, count, run_body, 0)
+        body(0)
+        lax.fori_loop(2, count, run_body, 0)
 
     barrier = pltpu.get_barrier_semaphore()
     peers(
@@ -388,6 +388,9 @@
             bring_own(a).start()
 
         def start(o):
+            for a in pair:
+                if a > 1:
+                    bring(a - 2, target(o), me).wait_send()
             for a in pair:
                 bring(a, target(o), me).start()
 
@@ -461,12 +464,12 @@
     def attend(o, carry):
         s = source(o)
 
-        @pl.when(o != half)
+        @pl.when(o != 1)
         def _():
             bring(2, s, s).wait_recv()
             bring(3, s, s).wait_recv()
 
-        @pl.when(o == half)
+        @pl.when(o == 1)
         def _():
             bring_own(2).wait()
             bring_own(3).wait()
@@ -477,11 +480,11 @@
 
         lax.fori_loop(0, each, inner, 0)
 
-        @pl.when(o != half)
+        @pl.when(o != 1)
         def _():
             give(0, s, me).start()
 
-        @pl.when(o == half)
+        @pl.when(o == 1)
         def _():
             give_own(0).start()
 
@@ -509,11 +512,11 @@
 
             lax.fori_loop(0, each, inner, 0)
 
-            @pl.when(o != half)
+            @pl.when(o != 1)
             def _():
                 give(a, s, me).start()
 
-            @pl.when(o == half)
+            @pl.when(o == 1)
             def _():
                 give_own(a).start()
 
@@ -521,7 +524,7 @@
 
         lax.fori_loop(0, count, finish, 0)
 
-    for a in range(4):
+    for a in (2, 3):
         peers(lambda o: bring(a, target(o), me).wait_send())
     for a in range(3):
         give_own(a).wait()

time: 379 us -> 343 us (0.905)
  the two profiles are of different devices: /device:TPU:27 before, /device:TPU:1 now
where the time goes in v1:
time: 343 us
  Pallas kernels  331 us (97%)
  local copies, waits for them, and re-layouts  8.19 us (2%)
    pallas_call x1, Pallas kernels, attend_by_head(): pl.pallas_call(head_kernel, in_specs=[pl.BlockSpec(memory_space=pltpu.SME...  331 us
    unnamed x8, local copies, waits for them, and re-layouts  7.72 us

profile of v1, /device:TPU:1, one launch (start us, length us, event | category | flops | bytes accessed | tf_op | source)
XLA Modules:
  0.0 343.1 jit_solution(8517215986974170070)
XLA Ops:
  0.6 0.7 multiply_add_fusion
  1.3 0.1 copy.14
  1.4 0.1 reshape.67
  1.6 0.1 fusion.2
  1.7 0.1 convert_reduce_fusion.2
  1.8 0.2 convert_reduce_fusion
  2.1 0.2 select_reduce_fusion
  2.3 0.8 copy.13
  3.1 0.1 reshape.66
  3.2 0.7 pad_add_fusion.tab_ref
  3.9 0.1 fusion.1
  4.0 0.1 reshape.75
  4.1 0.7 add_convert_fusion.wt_ref
  4.7 331.4 %head_attention.1 = (bf16[2,128,4096]{2,1,0:T(8,128)(2,1)}, bf16[2,128,4096]{2,1,0:T(8,128)(2,1)}, bf16[2,128,4096]{2,1,0:T(8,128)(2,1)}) custom-call(s32[576]{0:T(1024)} %pad_add_fusion.tab_ref, f32[768]{0:T(1024)} %add_convert_fusion.wt_ref, bf16[2,128,4096]{2,1,0:T(8,128)(2,1)} %bitcast.7, bf16[2,128,4096]{2,1,0:T(8,128)(2,1)} %bitcast.8, ...), custom_call_target="tpu_custom_call" | custom-call | tf_op jit(solution)/shard_map/head_attention/pallas_call | solution.py:569
  336.1 0.0 copy-start.1
  336.1 3.3 copy.18
  339.4 0.0 copy-done.1
  339.4 0.0 copy-start
  339.4 1.3 copy.19
  340.7 1.0 copy-done
  341.7 1.3 copy.20
  (5 shorter events, 0.0 us)
Async XLA Ops:
  336.1 3.3 copy-start.1
  339.4 2.3 copy-start

commit v2 on v1

--- a/solution.py
+++ b/solution.py
@@ -270,9 +270,24 @@
     )(idx, *incoming, *extra)
 
 
+HEAD_VMEM = 48 * 1024 * 1024
+
+
+def store_kernel(*refs):
+    sems = refs[6]
+    copies = [pltpu.make_async_copy(refs[m], refs[3 + m], sems.at[m]) for m in range(3)]
+    for copy in copies:
+        copy.start()
+    for copy in copies:
+        copy.wait()
+
+
 def head_kernel(
-    tab_ref,
-    wt_ref,
+    owner_ref,
+    within_ref,
+    global_ref,
+    owner_vec,
+    within_vec,
     k_in,
     v_in,
     q_in,
@@ -285,8 +300,6 @@
     qb,
     gb,
     dqb,
-    dkb,
-    dvb,
     dka,
     dva,
     terms_k,
@@ -294,6 +307,9 @@
     run,
     kcat,
     vcat,
+    sorted_ref,
+    last_ref,
+    has_ref,
     in_send,
     in_recv,
     out_send,
@@ -307,11 +323,13 @@
     each = k_in.shape[0]
     blocks = count * each
     entries = blocks * RAND
-    at_gid, at_rid = 0, blocks * GLOB
-    at_perm = at_rid + entries
-    at_last = at_perm + entries
-    at_carry = blocks * GLOB * NGLOB
-    at_has = at_carry + entries
+    per_owner = lax.div(blocks, lax.axis_size("ctx"))
+
+    def named_of(i, r):
+        return owner_ref[r, i] * per_owner + within_ref[r, i]
+
+    def same(a, b):
+        return (1 - jnp.minimum(jnp.abs(a - b), 1)).astype(jnp.float32)
 
     def side(o):
         return lax.rem(mine + 1 + o, 2) * half
@@ -335,7 +353,7 @@
         return pl.ds(pl.multiple_of(s * HEAD_DIM, HEAD_DIM), HEAD_DIM)
 
     ins = ((k_in, kb, rows_padded), (v_in, vb, rows_padded), (q_in, qb, rows_of), (g_in, gb, rows_of))
-    outs = ((dqb, dq_out), (dvb, dv_out), (dkb, dk_out))
+    outs = ((dqb, dq_out), (qb, dv_out), (gb, dk_out))
 
     def bring(a, t, s):
         x, y, rows = ins[a]
@@ -383,7 +401,37 @@
     )
     pl.semaphore_wait(barrier, count - 1)
 
+    def build_lists():
+        named = owner_vec[...] * per_owner + within_vec[...]
+        place = lax.broadcasted_iota(jnp.int32, named.shape, 0) * blocks
+        place += lax.broadcasted_iota(jnp.int32, named.shape, 1)
+        order = named * entries + place
+        rank = jnp.zeros_like(order)
+        for r in range(RAND):
+
+            def count_below(i, rank):
+                mark = named_of(i, r) * entries + r * blocks + i
+                return rank + jnp.minimum(jnp.maximum(order - mark, 0), 1)
+
+            rank = lax.fori_loop(0, blocks, count_below, rank)
+
+        def sort_step(e, carry):
+            sorted_ref[e] = jnp.sum(jnp.where(rank == e, order, 0))
+            return carry
+
+        lax.fori_loop(0, entries, sort_step, 0)
+
+        def span_step(j, carry):
+            upto = jnp.sum(jnp.where(named <= j, 1, 0))
+            last_ref[j] = jnp.maximum(upto - 1, 0)
+            has_ref[j] = jnp.minimum(jnp.sum(jnp.where(named == j, 1, 0)), 1)
+            return carry
+
+        lax.fori_loop(0, blocks, span_step, 0)
+
     for pair in ((0, 1), (2, 3)):
+        if pair == (2, 3):
+            build_lists()
         for a in pair:
             bring_own(a).start()
 
@@ -412,12 +460,12 @@
             at = slice(n * BLOCK, (n + 1) * BLOCK)
             kcat[at] = kb[i + n]
             vcat[at] = vb[i + n]
-        gids = [tab_ref[at_gid + i * GLOB + n] for n in range(GLOB)]
+        gids = [global_ref[n, i] for n in range(GLOB)]
         for n in range(GLOB + RAND):
             if n < GLOB:
                 named = gids[n]
             else:
-                named = tab_ref[at_rid + i * RAND + n - GLOB]
+                named = named_of(i, n - GLOB)
             at = slice((3 + n) * BLOCK, (4 + n) * BLOCK)
             kcat[at] = kb[named + 1]
             vcat[at] = vb[named + 1]
@@ -454,12 +502,12 @@
                 total = acc[m + 1]
                 for n in range(GLOB):
                     at = slice((3 + n) * BLOCK, (4 + n) * BLOCK)
-                    total += x[at] * wt_ref[((i * GLOB + n) * NGLOB) + m]
+                    total += x[at] * same(gids[n], m)
                 acc[m + 1] = total
         for n in range(RAND):
             at = slice((3 + GLOB + n) * BLOCK, (4 + GLOB + n) * BLOCK)
-            terms_k[i * RAND + n] = dk[at].astype(jnp.bfloat16)
-            terms_v[i * RAND + n] = dv[at].astype(jnp.bfloat16)
+            terms_k[n * blocks + i] = dk[at].astype(jnp.bfloat16)
+            terms_v[n * blocks + i] = dv[at].astype(jnp.bfloat16)
 
     def attend(o, carry):
         s = source(o)
@@ -492,21 +540,25 @@
 
     lax.fori_loop(0, count, attend, 0)
 
-    for a, terms, acc, low in ((1, terms_v, dva, dvb), (2, terms_k, dka, dkb)):
-
-        def scan(e, total):
-            total = total * wt_ref[at_carry + e] + terms[tab_ref[at_perm + e]].astype(jnp.float32)
+    for a, terms, acc, low in ((1, terms_v, dva, qb), (2, terms_k, dka, gb)):
+
+        def scan(e, carry):
+            total, before = carry
+            block = lax.div(sorted_ref[e], entries)
+            term = terms[lax.rem(sorted_ref[e], entries)].astype(jnp.float32)
+            total = total * same(block, before) + term
             run[e] = total
-            return total
-
-        lax.fori_loop(0, entries, scan, jnp.zeros((BLOCK, HEAD_DIM), jnp.float32))
+            return total, block
+
+        none = jnp.zeros((BLOCK, HEAD_DIM), jnp.float32)
+        lax.fori_loop(0, entries, scan, (none, jnp.int32(0)))
 
         def finish(o, carry):
             s = source(o)
 
             def inner(b, c):
                 j = s * each + b
-                total = run[tab_ref[at_last + j]] * wt_ref[at_has + j]
+                total = run[last_ref[j]] * has_ref[j].astype(jnp.float32)
                 low[j] = (total + acc[j + 1]).astype(jnp.bfloat16)
                 return c
 
@@ -543,39 +595,22 @@
     blocks = rows // BLOCK
     entries = blocks * RAND
     low = jnp.bfloat16
-    per_owner = blocks // lax.axis_size("ctx")
-    named = (random_owner * per_owner + random_within).reshape(-1)
-    ids = jnp.arange(entries, dtype=jnp.int32)
-    order = named * entries + ids
-    rank = jnp.sum((order[None, :] < order[:, None]).astype(jnp.int32), axis=1)
-    hit = rank[None, :] == ids[:, None]
-    perm = jnp.sum(jnp.where(hit, ids[None, :], 0), axis=1)
-    before = jnp.sum((named[None, :] < named[:, None]).astype(jnp.int32), axis=1)
-    start = jnp.sum(jnp.where(hit & (before == rank)[None, :], 1, 0), axis=1)
-    keys_at = jnp.arange(blocks, dtype=jnp.int32)
-    last = jnp.sum((named[None, :] <= keys_at[:, None]).astype(jnp.int32), axis=1) - 1
-    has = jnp.any(named[None, :] == keys_at[:, None], axis=1).astype(jnp.int32)
-    tab = jnp.concatenate(
-        [global_ids.reshape(-1), named, perm, jnp.maximum(last, 0)]
-    ).astype(jnp.int32)
-    tops = jnp.arange(NGLOB, dtype=jnp.int32)
-    picks = (global_ids.reshape(-1)[:, None] == tops).astype(jnp.int32).reshape(-1)
-    weights = jnp.concatenate([picks, 1 - start, has]).astype(jnp.float32)
     any_spec = pl.BlockSpec(memory_space=pl.ANY)
+    smem_spec = pl.BlockSpec(memory_space=pltpu.SMEM)
+    vmem_spec = pl.BlockSpec(memory_space=pltpu.VMEM)
+    owner, within, named = random_owner.T, random_within.T, global_ids.T
     vmem = pltpu.VMEM
     held = lambda n, dtype: vmem((n, BLOCK, HEAD_DIM), dtype)
     in_blocks = lambda x: x.reshape(tokens // BLOCK, BLOCK, width)
     dma = pltpu.SemaphoreType.DMA
     outs = pl.pallas_call(
         head_kernel,
-        in_specs=[pl.BlockSpec(memory_space=pltpu.SMEM)] * 2 + [any_spec] * 4,
-        out_specs=[any_spec] * 3,
-        out_shape=[jax.ShapeDtypeStruct((tokens // BLOCK, BLOCK, width), low)] * 3,
+        in_specs=[smem_spec] * 3 + [vmem_spec] * 2 + [any_spec] * 4,
+        out_specs=[vmem_spec] * 3,
+        out_shape=[vmem((tokens // BLOCK, BLOCK, width), low)] * 3,
         scratch_shapes=[
             held(blocks + 2, low),
             held(blocks + 2, low),
-            held(blocks, low),
-            held(blocks, low),
             held(blocks, low),
             held(blocks, low),
             held(blocks, low),
@@ -586,16 +621,28 @@
             held(entries, jnp.float32),
             vmem((SLOTS * BLOCK, HEAD_DIM), low),
             vmem((SLOTS * BLOCK, HEAD_DIM), low),
+            pltpu.SMEM((entries,), jnp.int32),
+            pltpu.SMEM((blocks,), jnp.int32),
+            pltpu.SMEM((blocks,), jnp.int32),
             dma((4, count)),
             dma((4, count)),
             dma((3, count)),
             dma((3, count)),
         ],
         compiler_params=pltpu.CompilerParams(
-            collective_id=0, has_side_effects=True, vmem_limit_bytes=VMEM_LIMIT
+            collective_id=0, has_side_effects=True, vmem_limit_bytes=HEAD_VMEM
         ),
         name="head_attention",
-    )(tab, weights, *[in_blocks(x) for x in (keys, values, query, grad_out)])
+    )(owner, within, named, owner, within, *[in_blocks(x) for x in (keys, values, query, grad_out)])
+    outs = pl.pallas_call(
+        store_kernel,
+        in_specs=[vmem_spec] * 3,
+        out_specs=[any_spec] * 3,
+        out_shape=[jax.ShapeDtypeStruct((tokens // BLOCK, BLOCK, width), low)] * 3,
+        scratch_shapes=[dma((3,))],
+        compiler_params=pltpu.CompilerParams(vmem_limit_bytes=2 * 1024 * 1024),
+        name="store",
+    )(*outs)
     return tuple(x.reshape(tokens, width) for x in outs)
 
 

time: 343 us -> 335 us (0.977)
  local copies, waits for them, and re-layouts: 8.19 us -> 0 us
    unnamed x8 -> x0, local copies, waits for them, and re-layouts: 7.72 us -> none
    pallas_call x1 -> x2, Pallas kernels: 331 us -> 334 us  [the longest x1 332 us: attend_by_head(): pl.pallas_call(head_kernel, in_specs=[smem_spec] * 3 + [vmem_spec] * 2 +...]
where the time goes in v2:
time: 335 us
  Pallas kernels  334 us (100%)
    pallas_call x1, Pallas kernels, attend_by_head(): pl.pallas_call(head_kernel, in_specs=[smem_spec] * 3 + [vmem_spec] * 2 +...  332 us

profile of v2, /device:TPU:1, one launch (start us, length us, event | category | flops | bytes accessed | tf_op | source)
XLA Modules:
  0.0 335.0 jit_solution(17117082225343820410)
XLA Ops:
  0.6 331.6 %head_attention.1 = (bf16[2,128,4096]{2,1,0:T(8,128)(2,1)S(1)}, bf16[2,128,4096]{2,1,0:T(8,128)(2,1)S(1)}, bf16[2,128,4096]{2,1,0:T(8,128)(2,1)S(1)}) custom-call(s32[3,64]{1,0:T(4,128)} %bitcast.14, s32[3,64]{1,0:T(4,128)} %bitcast.16, s32[2,64]{1,0:T(2,128)} %bitcast.18, s32[3,64]{1,0:T(4,128)} %bitcast.15, s32[3,64]{1,0:T(4,128)} %bitcast.17, ...), custom_call_target="tpu_custom_call" | custom-call | tf_op jit(solution)/shard_map/head_attention/pallas_call | solution.py:606
  332.2 2.7 store.1
